TPU v7x, 32 devices: a whole 2x2x4 slice. The times are simulated.
32 devices in a mesh: groups: 2 (over x), tensor: 8 (over z, y), dp: 2 (over core).
Axes of the slice: x: 2, y: 2, z: 4, core: 2. Of those that a mesh axis runs over, the one named last changes fastest.
Arguments:
- inputs: bfloat16 [4, 256, 16384], P(('groups', 'dp'), None, 'tensor'), parts along dimension 0, may hold values from -6 to 6
- cross_w: bfloat16 [16384, 16384], P('dp', 'tensor'), may hold values from -0.046875 to 0.046875
- cross_b: float32 [16384], P('tensor'), may hold values from -3 to 3
- mix_weight: bfloat16 [128, 512], replicated, may hold values from -0.5 to 0.5
- mix_bias: float32 [512], replicated, may hold values from -3 to 3
- out_weight: bfloat16 [512, 128], replicated, may hold values from -0.25 to 0.25
- cotangent: bfloat16 [4, 256, 16384], P(('groups', 'dp'), 'tensor'), parts along dimension 0, may hold values from -12 to 12
Outputs:
- compressed: bfloat16 [4, 256, 16384], P(('groups', 'dp'), 'tensor'), parts along dimension 0
- grad_inputs: bfloat16 [4, 256, 16384], P(('groups', 'dp'), None, 'tensor'), parts along dimension 0
- grad_mix: float32 [256, 512], P('groups'), parts along dimension 0
- grad_mix_bias: float32 [1024], P('groups'), parts along dimension 0
- grad_out: float32 [1024, 128], P('groups'), parts along dimension 0
There are 2 independent parts, one for each index of `groups`. A program takes and returns all parts, laid end to end along the dimension named above; an argument that names none is the same for every part. Nothing has to cross between parts.
All inputs are finite; a program needn't handle non-finite values.
Results may differ from a plain program's by a relative error of at most 0.019.
Values may be sent and summed in bfloat16 or wider, within the bound.
No kernel may reach another device: no remote copies, remote signals or barrier semaphores. Data moves between devices by JAX's collectives and lax.ppermute only.
A program may use at most 256 MiB of HBM per device.

v0:
```python
import jax
import jax.numpy as jnp
from jax import lax
from jax.sharding import PartitionSpec as P

F = 128
E = 128
K = 128


def shards(inputs, cross_w, cross_b, mix_weight, mix_bias, out_weight, cotangent):
    local_rows = inputs[0]
    dp_count = lax.axis_size("dp")
    full_rows = lax.all_gather(local_rows, "tensor", axis=1, tiled=True)
    linear = jnp.dot(
        full_rows,
        lax.all_gather(cross_w, "dp", axis=0, tiled=True),
        preferred_element_type=jnp.float32,
    )
    linear = linear + cross_b
    base_rows = local_rows.astype(jnp.float32)
    crossed = (base_rows * linear + base_rows).astype(jnp.bfloat16)
    owned = lax.all_to_all(crossed, "tensor", split_axis=0, concat_axis=1, tiled=True)
    owned_count = owned.shape[0]
    grid_rows = owned.reshape(owned_count, F, E)
    gram_rows = (
        jnp.einsum("bfe,bge->bfg", grid_rows, grid_rows, preferred_element_type=jnp.float32) / E
    ).astype(jnp.bfloat16)
    pre_act = (
        jnp.einsum("bfg,gh->bfh", gram_rows, mix_weight, preferred_element_type=jnp.float32)
        + mix_bias
    )
    sigmoid_pre = jax.nn.sigmoid(pre_act)
    hidden = (pre_act * sigmoid_pre).astype(jnp.bfloat16)
    compressed = jnp.einsum(
        "bfh,hk->bfk", hidden, out_weight, preferred_element_type=jnp.float32
    ).astype(jnp.bfloat16)
    upstream = cotangent[0].reshape(owned_count, F, K)
    d_hidden = jnp.einsum("bfk,hk->bfh", upstream, out_weight, preferred_element_type=jnp.float32)
    out_term = jnp.einsum("bfh,bfk->hk", hidden, upstream, preferred_element_type=jnp.float32)
    d_pre = (d_hidden * sigmoid_pre * (1.0 + pre_act * (1.0 - sigmoid_pre))).astype(jnp.bfloat16)
    mix_term = jnp.einsum("bfg,bfh->gh", gram_rows, d_pre, preferred_element_type=jnp.float32)
    bias_term = jnp.sum(d_pre.astype(jnp.float32), axis=(0, 1))
    mix_sum, bias_sum, out_sum = (
        lax.psum(mix_term.astype(jnp.bfloat16), ("tensor", "dp")).astype(jnp.float32),
        lax.psum(bias_term.astype(jnp.bfloat16), ("tensor", "dp")).astype(jnp.float32),
        lax.psum(out_term.astype(jnp.bfloat16), ("tensor", "dp")).astype(jnp.float32),
    )
    row_total = owned_count * lax.axis_size("tensor") * dp_count
    d_gram = jnp.einsum("bfh,gh->bfg", d_pre, mix_weight, preferred_element_type=jnp.float32)
    grid_wide = grid_rows.astype(jnp.float32)
    d_grid = jnp.einsum("bfg,bge->bfe", d_gram + jnp.swapaxes(d_gram, 1, 2), grid_wide) / E
    d_owned = d_grid.astype(jnp.bfloat16).reshape(owned_count, F * E)
    d_crossed = lax.all_to_all(d_owned, "tensor", split_axis=1, concat_axis=0, tiled=True)
    d_crossed_wide = d_crossed.astype(jnp.float32)
    d_linear = (d_crossed_wide * base_rows).astype(jnp.bfloat16)
    contract = (((1,), (1,)), ((), ()))
    back_terms = lax.dot_general(
        d_linear,
        lax.all_gather(cross_w, "dp", axis=0, tiled=True),
        contract,
        preferred_element_type=jnp.float32,
    )
    back_sum = lax.psum_scatter(
        back_terms.astype(jnp.bfloat16), "tensor", scatter_dimension=1, tiled=True
    ).astype(jnp.float32)
    grad_inputs = (d_crossed_wide * (linear + 1.0) + back_sum).astype(jnp.bfloat16)
    return (
        compressed.reshape(1, owned_count, F * K),
        grad_inputs[None],
        mix_sum / row_total,
        bias_sum / row_total,
        out_sum / row_total,
    )


def solution(mesh):
    return jax.shard_map(
        shards,
        mesh=mesh,
        in_specs=(
            P(("groups", "dp"), None, "tensor"),
            P("dp", "tensor"),
            P("tensor"),
            P(),
            P(),
            P(),
            P(("groups", "dp"), "tensor", None),
        ),
        out_specs=(
            P(("groups", "dp"), "tensor", None),
            P(("groups", "dp"), None, "tensor"),
            P("groups", None),
            P("groups"),
            P("groups", None),
        ),
        check_vma=False,
    )
```

profile of v0, /device:TPU:0, one launch (start us, length us, event | category | flops | bytes accessed | tf_op | source)
XLA Modules:
  0.0 582.4 jit_solution(2011968667886465584)
XLA Ops:
  7.2 0.0 copy-start
  7.2 0.0 all-gather.6.cloned.1.call-start
  7.2 0.7 all-gather.6.cloned.1.call-update
  7.9 0.0 copy-start.2
  7.9 0.0 copy-start.11
  7.9 0.0 all-gather.4.cloned.1.call-start
  8.0 0.7 all-gather.4.cloned.1.call-update
  8.7 129.2 %all-gather.6.cloned.1.call-done = bf16[1,256,16384]{2,1,0:T(8,128)(2,1)} async-done(((bf16[1,256,2048]{2,1,0:T(8,128)(2,1)}), bf16[1,256,16384]{2,1,0:T(8,128)(2,1)}) %all-gather.6.cloned.1.call-update) | async-done | bytes 8388624 | tf_op jit(solution)/shard_map/all_gather | solution.py:14
  137.9 94.9 %all-gather.4.cloned.1.call-done = bf16[16384,2048]{1,0:T(8,128)(2,1)} async-done(((bf16[8192,2048]{1,0:T(8,128)(2,1)}), bf16[16384,2048]{1,0:T(8,128)(2,1)}) %all-gather.4.cloned.1.call-update) | async-done | bytes 67108880 | tf_op jit(solution)/shard_map/all_gather | solution.py:17
  232.7 0.0 copy-done.2
  232.7 29.4 %fusion.5 = (bf16[256,2048]{1,0:T(8,128)(2,1)}, f32[256,2048]{1,0:T(8,128)}) fusion(bf16[1,256,2048]{2,1,0:T(8,128)(2,1)S(1)} %copy-done.2, f32[2048]{0:T(1024)S(1)} %copy-done.11, bf16[16384,2048]{1,0:T(8,128)(2,1)} %all-gather.4.cloned.1.call-done, bf16[1,256,16384]{2,1,0:T(8,128)(2,1)} %all-gather.6.cloned.1.call-done), kind=kOutput, calls=%fused_computation.10 | convolution fusion | flops 17182490624 | bytes 79699968 | tf_op jit(solution)/shard_map/dot_general | solution.py:15
  262.2 5.8 all-to-all-start
  267.9 0.2 copy.19
  268.2 0.0 copy-start.12
  268.2 26.0 %all-to-all-done = bf16[8,32,2048]{2,1,0:T(8,128)(2,1)S(1)} async-done(((bf16[8,32,2048]{2,1,0:T(8,128)(2,1)}), bf16[8,32,2048]{2,1,0:T(8,128)(2,1)S(1)}, u32[]{:S(2)}, u32[]{:S(2)}) %all-to-all-start) | async-done | bytes 1048608 | tf_op jit(solution)/shard_map/all_to_all | solution.py:23
  294.2 0.6 copy.12
  294.7 0.5 reshape.29
  295.3 0.8 multiply_convert_fusion.3
  296.1 0.0 copy-start.5
  296.2 0.0 copy-start.10
  296.2 3.9 multiply_convert_fusion.1
  300.1 0.0 copy-done.5
  300.1 3.7 fusion.18
  303.8 2.0 copy-done.1
  305.7 1.2 fusion.14
  307.0 1.8 copy.13
  308.8 3.0 multiply_convert_fusion.2
  311.8 1.6 all_to_all.25
  313.4 1.5 copy.14
  315.0 3.8 all-to-all-start.1
  318.8 0.2 all-reduce.3.cloned.1.call-start
  319.0 3.7 fusion.10
  322.8 2.0 fusion.11
  324.7 0.0 all-reduce.3.cloned.1.call-update
  324.8 0.0 reduce-scatter.2.cloned.1.call-start
  324.8 20.7 %all-to-all-done.1 = bf16[32,8,2048]{2,0,1:T(8,128)(2,1)S(1)} async-done(((bf16[32,8,2048]{2,0,1:T(8,128)(2,1)}), bf16[32,8,2048]{2,0,1:T(8,128)(2,1)S(1)}, u32[]{:S(2)}, u32[]{:S(2)}) %all-to-all-start.1) | async-done | bytes 1048608 | tf_op jit(solution)/shard_map/all_to_all | solution.py:54
  345.5 0.4 fusion.6
  345.9 30.1 %convolution_convert_fusion = bf16[256,16384]{1,0:T(8,128)(2,1)} fusion(bf16[256,2048]{1,0:T(8,128)(2,1)S(1)} %fusion.6, bf16[16384,2048]{1,0:T(8,128)(2,1)} %all-gather.4.cloned.1.call-done), kind=kOutput, calls=%fused_computation | convolution fusion | flops 17184063488 | bytes 76546048 | tf_op jit(solution)/shard_map/dot_general | solution.py:58
  376.0 0.0 reduce-scatter.2.cloned.1.call-update
  376.0 3.4 convolution_convert_fusion.1
  379.4 1.3 reshape.30
  380.7 31.5 %psum.22 = bf16[512]{0:T(512)(128)(2,1)S(1)} all-reduce(bf16[512]{0:T(512)(128)(2,1)S(1)} %get-tuple-element.11), channel_id=1, replica_groups=mesh['groups'=2,'tensor'=8,'dp'=2] {'tensor','dp'}, use_global_device_ids=true, to_apply=%region_3.0 | all-reduce | flops 512 | bytes 2048 | tf_op jit(solution)/shard_map/psum | solution.py:46
  412.2 0.6 convert_multiply_fusion.4
  412.8 6.3 %all-reduce.3.cloned.1.call-done = (bf16[128,512]{1,0:T(8,128)(2,1)}, bf16[512,128]{1,0:T(8,128)(2,1)}) async-done(((bf16[128,512]{1,0:T(8,128)(2,1)}, bf16[512,128]{1,0:T(8,128)(2,1)}), (bf16[128,512]{1,0:T(8,128)(2,1)}, bf16[512,128]{1,0:T(8,128)(2,1)})) %all-reduce.3.cloned.1.call-update) | async-done | bytes 262160 | tf_op jit(solution)/shard_map/psum | solution.py:45
  419.1 1.6 convert_multiply_fusion.3
  420.8 1.6 convert_multiply_fusion.2
  422.4 150.2 %reduce-scatter.2.cloned.1.call-done = bf16[256,2048]{1,0:T(8,128)(2,1)} async-done(((bf16[256,16384]{1,0:T(8,128)(2,1)}), bf16[256,2048]{1,0:T(8,128)(2,1)}) %reduce-scatter.2.cloned.1.call-update) | async-done | bytes 1048592 | tf_op jit(solution)/shard_map/reduce_scatter | solution.py:64
  572.5 3.3 fusion.8
  (17 shorter events, 0.0 us)
Async XLA Ops:
  7.2 289.0 %copy-start = (bf16[128,512]{1,0:T(8,128)(2,1)S(1)}, bf16[128,512]{1,0:T(8,128)(2,1)}, u32[]{:S(2)}) copy-start(bf16[128,512]{1,0:T(8,128)(2,1)} %param.10) | copy-start | bytes 393220
  7.2 130.7 %all-gather.6.cloned.1.call-start = ((), (), s32[]{:S(2)}) async-start(), calls=%async_computation.5 | async-start | bytes 9437184 | tf_op jit(solution)/shard_map/all_gather | solution.py:14
  7.9 224.8 %copy-start.2 = (bf16[1,256,2048]{2,1,0:T(8,128)(2,1)S(1)}, bf16[1,256,2048]{2,1,0:T(8,128)(2,1)}, u32[]{:S(2)}) copy-start(bf16[1,256,2048]{2,1,0:T(8,128)(2,1)} %param.7) | copy-start | bytes 3145732
  7.9 224.8 %copy-start.11 = (f32[2048]{0:T(1024)S(1)}, f32[2048]{0:T(1024)}, u32[]{:S(2)}) copy-start(f32[2048]{0:T(1024)} %param.9) | copy-start | bytes 24580
  7.9 224.8 %all-gather.4.cloned.1.call-start = ((), (), s32[]{:S(2)}) async-start(), calls=%async_computation.3 | async-start | bytes 100663296 | tf_op jit(solution)/shard_map/all_gather | solution.py:17
  8.7 259.2 %copy-start.7 = (bf16[1,32,16384]{2,1,0:T(8,128)(2,1)S(1)}, bf16[1,32,16384]{2,1,0:T(8,128)(2,1)}, u32[]{:S(2)}) copy-start(bf16[1,32,16384]{2,1,0:T(8,128)(2,1)} %param.13) | copy-start | bytes 3145732
  262.2 32.0 %all-to-all-start = ((bf16[8,32,2048]{2,1,0:T(8,128)(2,1)}), bf16[8,32,2048]{2,1,0:T(8,128)(2,1)S(1)}, u32[]{:S(2)}, u32[]{:S(2)}) async-start(bf16[8,32,2048]{2,1,0:T(8,128)(2,1)} %bitcast.2), calls=%async_computation | async-start | bytes 2097152 | tf_op jit(solution)/shard_map/all_to_all | solution.py:23
  268.2 31.9 %copy-start.8 = (bf16[4,8,128,128]{3,2,1,0:T(8,128)(2,1)}, bf16[4,8,128,128]{3,2,1,0:T(8,128)(2,1)S(1)}, u32[]{:S(2)}) copy-start(bf16[4,8,128,128]{3,2,1,0:T(8,128)(2,1)S(1)} %copy.19) | copy-start | bytes 3145732
  268.2 27.9 %copy-start.12 = (f32[512]{0:T(512)S(1)}, f32[512]{0:T(512)}, u32[]{:S(2)}) copy-start(f32[512]{0:T(512)} %param.11) | copy-start | bytes 6148
  296.1 3.9 copy-start.5
  296.2 3.9 copy-start.10
  303.8 2.0 copy-start.1
  311.8 7.2 %copy-start.6 = (bf16[32,128,128]{2,1,0:T(8,128)(2,1)S(1)}, bf16[32,128,128]{2,1,0:T(8,128)(2,1)}, u32[]{:S(2)}) copy-start(bf16[32,128,128]{2,1,0:T(8,128)(2,1)} %copy-done.5) | copy-start | bytes 3145732
  315.0 7.8 %copy-start.9 = (bf16[4,8,128,128]{3,2,1,0:T(8,128)(2,1)S(1)}, bf16[4,8,128,128]{3,2,1,0:T(8,128)(2,1)}, u32[]{:S(2)}) copy-start(bf16[4,8,128,128]{3,2,1,0:T(8,128)(2,1)} %copy-done.8) | copy-start | bytes 3145732
  315.0 30.5 %all-to-all-start.1 = ((bf16[32,8,2048]{2,0,1:T(8,128)(2,1)}), bf16[32,8,2048]{2,0,1:T(8,128)(2,1)S(1)}, u32[]{:S(2)}, u32[]{:S(2)}) async-start(bf16[32,8,2048]{2,0,1:T(8,128)(2,1)} %copy.14), calls=%async_computation.1 | async-start | bytes 2097152 | tf_op jit(solution)/shard_map/all_to_all | solution.py:54
  318.8 100.4 %all-reduce.3.cloned.1.call-start = ((), (), s32[]{:S(2)}) async-start(), calls=%async_computation.6 | async-start | bytes 524288 | tf_op jit(solution)/shard_map/psum | solution.py:45
  319.0 3.8 copy-start.4
  322.8 22.8 %copy-start.3 = (bf16[1,256,2048]{2,1,0:T(8,128)(2,1)S(1)}, bf16[1,256,2048]{2,1,0:T(8,128)(2,1)}, u32[]{:S(2)}) copy-start(bf16[1,256,2048]{2,1,0:T(8,128)(2,1)} %param.7) | copy-start | bytes 3145732
  324.8 247.8 %reduce-scatter.2.cloned.1.call-start = ((), (), s32[]{:S(2)}) async-start(), calls=%async_computation.4 | async-start | bytes 9437184 | tf_op jit(solution)/shard_map/reduce_scatter | solution.py:64
Sparse Core Ops, SparseCore 0:
  10.2 127.6 all-gather.5
  139.4 93.2 all-gather.3
  324.9 94.2 all-reduce.2
  422.6 149.8 reduce-scatter.1
where the time goes:
time: 583 us; the launch traced here: 582 us
  waiting for transfers between devices  429 us (74%)
  matrix products  81.3 us (14%)
  blocking collectives  31.5 us (5%)
  between operations  13.9 us (2%)
  starting transfers between devices  9.88 us (2%)
  local copies, waits for them, and re-layouts  9.63 us (2%)
  other arithmetic  7.58 us (1%)
    reduce_scatter x1, waiting for transfers between devices, shards(): lax.psum_scatter(back_terms.astype(jnp.bfloat16), 'tensor', scatter_dimen...  150 us
    all_gather x1, waiting for transfers between devices, shards(): full_rows = lax.all_gather(local_rows, 'tensor', axis=1, tiled=True)  129 us
    all_gather x1, waiting for transfers between devices, shards(): lax.all_gather(cross_w, 'dp', axis=0, tiled=True)  94.9 us
    psum x1, blocking collectives, shards(): lax.psum(bias_term.astype(jnp.bfloat16), ('tensor', 'dp'))  31.5 us
    dot_general x1, matrix products, shards(): lax.dot_general(d_linear, lax.all_gather(cross_w, 'dp', axis=0, tiled=Tru...  30.1 us
    dot_general x1, matrix products, shards(): jnp.dot(full_rows, lax.all_gather(cross_w, 'dp', axis=0, tiled=True), pre...  29.4 us
    all_to_all x1, waiting for transfers between devices, shards(): lax.all_to_all(crossed, 'tensor', split_axis=0, concat_axis=1, tiled=True)  26 us
    all_to_all x1, waiting for transfers between devices, shards(): lax.all_to_all(d_owned, 'tensor', split_axis=1, concat_axis=0, tiled=True)  20.7 us
  transfers between devices with their start and end apart: 6, of which 6 were waited for; matrix products, arithmetic and copies ran while one was open for 8% of the time, Pallas kernels for 0%

commit v1 on v0

--- a/solution.py
+++ b/solution.py
@@ -8,10 +8,21 @@
 K = 128
 
 
+def around_the_ring(x, axis, along):
+    size = lax.axis_size(axis)
+    right = [(i, (i + 1) % size) for i in range(size)]
+    shards = [x]
+    for reach in range(1, size):
+        shards = [lax.ppermute(shards[0], axis, right), *shards]
+    out = jnp.concatenate(shards, axis=along)
+    shift = (lax.axis_index(axis) + 1) * shards[-1].shape[along]
+    return jnp.roll(out, shift, axis=along)
+
+
 def shards(inputs, cross_w, cross_b, mix_weight, mix_bias, out_weight, cotangent):
     local_rows = inputs[0]
     dp_count = lax.axis_size("dp")
-    full_rows = lax.all_gather(local_rows, "tensor", axis=1, tiled=True)
+    full_rows = around_the_ring(local_rows, "tensor", 1)
     linear = jnp.dot(
         full_rows,
         lax.all_gather(cross_w, "dp", axis=0, tiled=True),

time: 583 us -> 554 us (0.950)
  waiting for transfers between devices: 429 us -> 370 us
  local copies, waits for them, and re-layouts: 9.63 us -> 37.8 us
    ppermute x0 -> x7, waiting for transfers between devices: none -> 175 us  [around_the_ring(): shards = [lax.ppermute(shards[0], axis, right), *shards]]
    all_gather x1 -> x0, waiting for transfers between devices: 129 us -> none  [shards(): full_rows = lax.all_gather(local_rows, 'tensor', axis=1, tiled=True)]
    all_gather x1, waiting for transfers between devices: 94.9 us -> 0.01 us  [shards(): lax.all_gather(cross_w, 'dp', axis=0, tiled=True)]
    unnamed x27 -> x50, local copies, waits for them, and re-layouts: 2.28 us -> 29.3 us
    all_to_all x1, waiting for transfers between devices: 26 us -> 19.4 us  [shards(): lax.all_to_all(crossed, 'tensor', split_axis=0, concat_axis=1, tiled=True)]
  transfers between devices with their start and end apart: 6 -> 12, of which waited for: 6 -> 11; matrix products, arithmetic and copies ran while one was open for 8% -> 13% of each run, Pallas kernels for 0% -> 0%
where the time goes in v1:
time: 554 us; the launch traced here: 553 us
  waiting for transfers between devices  370 us (67%)
  matrix products  83.8 us (15%)
  local copies, waits for them, and re-layouts  37.8 us (7%)
  blocking collectives  29.6 us (5%)
  between operations  13.9 us (3%)
  starting transfers between devices  10.8 us (2%)
  other arithmetic  7.58 us (1%)
    ppermute x7, waiting for transfers between devices, around_the_ring(): shards = [lax.ppermute(shards[0], axis, right), *shards]  175 us
    reduce_scatter x1, waiting for transfers between devices, shards(): lax.psum_scatter(back_terms.astype(jnp.bfloat16), 'tensor', scatter_dimen...  150 us
    dot_general x1, matrix products, shards(): lax.dot_general(d_linear, lax.all_gather(cross_w, 'dp', axis=0, tiled=Tru...  30.1 us
    psum x1, blocking collectives, shards(): lax.psum(bias_term.astype(jnp.bfloat16), ('tensor', 'dp'))  29.6 us
    dot_general x1, matrix products, shards(): jnp.dot(full_rows, lax.all_gather(cross_w, 'dp', axis=0, tiled=True), pre...  29.5 us
    unnamed x50, local copies, waits for them, and re-layouts  29.3 us
    all_to_all x1, waiting for transfers between devices, shards(): lax.all_to_all(crossed, 'tensor', split_axis=0, concat_axis=1, tiled=True)  19.4 us
    all_to_all x1, waiting for transfers between devices, shards(): lax.all_to_all(d_owned, 'tensor', split_axis=1, concat_axis=0, tiled=True)  15.2 us
  transfers between devices with their start and end apart: 12, of which 11 were waited for; matrix products, arithmetic and copies ran while one was open for 13% of the time, Pallas kernels for 0%

profile of v1, /device:TPU:0, one launch (start us, length us, event | category | flops | bytes accessed | tf_op | source)
XLA Modules:
  0.0 553.1 jit_solution(16784198843016085013)
XLA Ops:
  8.4 3.0 collective-permute-start
  11.4 26.2 %collective-permute-done = bf16[256,2048]{1,0:T(8,128)(2,1)S(1)} collective-permute-done((bf16[256,2048]{1,0:T(8,128)(2,1)S(1)}, bf16[256,2048]{1,0:T(8,128)(2,1)S(1)}, u32[]{:S(2)}, u32[]{:S(2)}) %collective-permute-start) | collective-permute-done | bytes 1048608 | tf_op jit(solution)/shard_map/ppermute | solution.py:16
  37.6 27.0 %collective-permute-done.1 = bf16[256,2048]{1,0:T(8,128)(2,1)S(1)} collective-permute-done((bf16[256,2048]{1,0:T(8,128)(2,1)S(1)}, bf16[256,2048]{1,0:T(8,128)(2,1)S(1)}, u32[]{:S(2)}, u32[]{:S(2)}) %collective-permute-start.1) | collective-permute-done | bytes 1048608 | tf_op jit(solution)/shard_map/ppermute | solution.py:16
  64.7 26.1 %collective-permute-done.2 = bf16[256,2048]{1,0:T(8,128)(2,1)S(1)} collective-permute-done((bf16[256,2048]{1,0:T(8,128)(2,1)S(1)}, bf16[256,2048]{1,0:T(8,128)(2,1)S(1)}, u32[]{:S(2)}, u32[]{:S(2)}) %collective-permute-start.2) | collective-permute-done | bytes 1048608 | tf_op jit(solution)/shard_map/ppermute | solution.py:16
  91.7 25.2 %collective-permute-done.3 = bf16[256,2048]{1,0:T(8,128)(2,1)S(1)} collective-permute-done((bf16[256,2048]{1,0:T(8,128)(2,1)S(1)}, bf16[256,2048]{1,0:T(8,128)(2,1)S(1)}, u32[]{:S(2)}, u32[]{:S(2)}) %collective-permute-start.3) | collective-permute-done | bytes 1048608 | tf_op jit(solution)/shard_map/ppermute | solution.py:16
  117.9 24.3 %collective-permute-done.4 = bf16[256,2048]{1,0:T(8,128)(2,1)S(1)} collective-permute-done((bf16[256,2048]{1,0:T(8,128)(2,1)S(1)}, bf16[256,2048]{1,0:T(8,128)(2,1)S(1)}, u32[]{:S(2)}, u32[]{:S(2)}) %collective-permute-start.4) | collective-permute-done | bytes 1048608 | tf_op jit(solution)/shard_map/ppermute | solution.py:16
  143.1 23.5 %collective-permute-done.5 = bf16[256,2048]{1,0:T(8,128)(2,1)} collective-permute-done((bf16[256,2048]{1,0:T(8,128)(2,1)S(1)}, bf16[256,2048]{1,0:T(8,128)(2,1)}, u32[]{:S(2)}, u32[]{:S(2)}) %collective-permute-start.5) | collective-permute-done | bytes 1048608 | tf_op jit(solution)/shard_map/ppermute | solution.py:16
  166.6 22.7 %collective-permute-done.6 = bf16[256,2048]{1,0:T(8,128)(2,1)} collective-permute-done((bf16[256,2048]{1,0:T(8,128)(2,1)}, bf16[256,2048]{1,0:T(8,128)(2,1)}, u32[]{:S(2)}, u32[]{:S(2)}) %collective-permute-start.6) | collective-permute-done | bytes 1048608 | tf_op jit(solution)/shard_map/ppermute | solution.py:16
  189.4 2.3 constant_dynamic-update-slice_fusion.15
  191.7 2.3 constant_dynamic-update-slice_fusion.14
  194.0 2.4 constant_dynamic-update-slice_fusion.13
  196.4 2.4 constant_dynamic-update-slice_fusion.12
  198.8 1.1 constant_dynamic-update-slice_fusion.11
  199.8 1.0 constant_dynamic-update-slice_fusion.10
  200.9 1.1 constant_dynamic-update-slice_fusion.9
  201.9 1.1 constant_dynamic-update-slice_fusion.8
  203.0 2.4 constant_dynamic-update-slice_fusion.7
  205.3 2.3 constant_dynamic-update-slice_fusion.6
  207.7 1.1 constant_dynamic-update-slice_fusion.5
  208.8 1.0 constant_dynamic-update-slice_fusion.4
  209.8 1.1 constant_dynamic-update-slice_fusion.3
  210.9 1.1 constant_dynamic-update-slice_fusion.2
  211.9 1.0 constant_dynamic-update-slice_fusion.1
  213.0 1.0 constant_dynamic-update-slice_fusion
  214.0 29.5 %fusion.6 = (bf16[256,2048]{1,0:T(8,128)(2,1)}, f32[256,2048]{1,0:T(8,128)}) fusion(bf16[1,256,2048]{2,1,0:T(8,128)(2,1)S(1)} %copy-done.2, f32[2048]{0:T(1024)S(1)} %copy-done.15, bf16[16384,2048]{1,0:T(8,128)(2,1)} %all-gather.2.cloned.1.call-done, bf16[256,32768]{1,0:T(8,128)(2,1)} %constant_dynamic-update-slice_fusion, s32[]{:T(128)S(6)} %select_n.14), kind=kOutput, calls=%fused_computation.10 | convolution fusion | flops 17182490624 | bytes 79699968 | tf_op jit(solution)/shard_map/dot_general | solution.py:26
  243.6 3.9 all-to-all-start
  247.7 19.4 %all-to-all-done = bf16[8,32,2048]{2,1,0:T(8,128)(2,1)S(1)} async-done(((bf16[8,32,2048]{2,1,0:T(8,128)(2,1)}), bf16[8,32,2048]{2,1,0:T(8,128)(2,1)S(1)}, u32[]{:S(2)}, u32[]{:S(2)}) %all-to-all-start) | async-done | bytes 1048608 | tf_op jit(solution)/shard_map/all_to_all | solution.py:34
  269.2 3.9 multiply_convert_fusion.1
  273.1 3.7 fusion.19
  276.8 2.0 copy-done.1
  278.7 1.3 fusion.14
  280.0 1.8 copy.13
  281.8 3.0 multiply_convert_fusion.2
  284.9 1.7 all_to_all.25
  286.5 1.5 copy.14
  288.1 3.6 all-to-all-start.1
  291.7 3.9 fusion.10
  295.7 4.1 fusion.11
  300.1 15.2 %all-to-all-done.1 = bf16[32,8,2048]{2,0,1:T(8,128)(2,1)S(1)} async-done(((bf16[32,8,2048]{2,0,1:T(8,128)(2,1)}), bf16[32,8,2048]{2,0,1:T(8,128)(2,1)S(1)}, u32[]{:S(2)}, u32[]{:S(2)}) %all-to-all-start.1) | async-done | bytes 1048608 | tf_op jit(solution)/shard_map/all_to_all | solution.py:65
  315.7 30.1 %convolution_convert_fusion = bf16[256,16384]{1,0:T(8,128)(2,1)} fusion(bf16[256,2048]{1,0:T(8,128)(2,1)S(1)} %fusion.5, bf16[16384,2048]{1,0:T(8,128)(2,1)} %all-gather.2.cloned.1.call-done), kind=kOutput, calls=%fused_computation | convolution fusion | flops 17184063488 | bytes 76546048 | tf_op jit(solution)/shard_map/dot_general | solution.py:69
  345.8 3.4 convolution_convert_fusion.1
  349.3 1.3 reshape.30
  350.6 29.6 %psum.22 = bf16[512]{0:T(512)(128)(2,1)S(1)} all-reduce(bf16[512]{0:T(512)(128)(2,1)S(1)} %get-tuple-element.11), channel_id=1, replica_groups=mesh['groups'=2,'tensor'=8,'dp'=2] {'tensor','dp'}, use_global_device_ids=true, to_apply=%region_3.4 | all-reduce | flops 512 | bytes 2048 | tf_op jit(solution)/shard_map/psum | solution.py:57
  380.7 8.9 %all-reduce.3.cloned.1.call-done = (bf16[128,512]{1,0:T(8,128)(2,1)}, bf16[512,128]{1,0:T(8,128)(2,1)}) async-done(((bf16[128,512]{1,0:T(8,128)(2,1)}, bf16[512,128]{1,0:T(8,128)(2,1)}), (bf16[128,512]{1,0:T(8,128)(2,1)}, bf16[512,128]{1,0:T(8,128)(2,1)})) %all-reduce.3.cloned.1.call-update) | async-done | bytes 262160 | tf_op jit(solution)/shard_map/psum | solution.py:56
  389.6 1.6 convert_multiply_fusion.1
  391.3 1.6 convert_multiply_fusion.2
  392.9 150.3 %reduce-scatter.2.cloned.1.call-done = bf16[256,2048]{1,0:T(8,128)(2,1)} async-done(((bf16[256,16384]{1,0:T(8,128)(2,1)}), bf16[256,2048]{1,0:T(8,128)(2,1)}) %reduce-scatter.2.cloned.1.call-update) | async-done | bytes 1048592 | tf_op jit(solution)/shard_map/reduce_scatter | solution.py:75
  543.2 3.3 fusion.8
  (52 shorter events, 7.7 us)
Async XLA Ops:
  7.2 262.0 %copy-start = (bf16[128,512]{1,0:T(8,128)(2,1)S(1)}, bf16[128,512]{1,0:T(8,128)(2,1)}, u32[]{:S(2)}) copy-start(bf16[128,512]{1,0:T(8,128)(2,1)} %param.10) | copy-start | bytes 393220
  7.2 1.3 copy-start.2
  7.2 206.8 %all-gather.2.cloned.1.call-start = ((), (), s32[]{:S(2)}) async-start(), calls=%async_computation.3 | async-start | bytes 100663296 | tf_op jit(solution)/shard_map/all_gather | solution.py:28
  8.4 29.2 %collective-permute-start = (bf16[256,2048]{1,0:T(8,128)(2,1)S(1)}, bf16[256,2048]{1,0:T(8,128)(2,1)S(1)}, u32[]{:S(2)}, u32[]{:S(2)}) collective-permute-start(bf16[256,2048]{1,0:T(8,128)(2,1)S(1)} %bitcast.61), channel_id=1, source_target_pairs={{0,2},{2,4},{4,6},{6,8},{8,10},{10,12},{12,14},{14,0},{1,3},{3,5},... | collective-permute-start | bytes 3145736 | tf_op jit(solution)/shard_map/ppermute | solution.py:16
  37.6 27.0 %collective-permute-start.1 = (bf16[256,2048]{1,0:T(8,128)(2,1)S(1)}, bf16[256,2048]{1,0:T(8,128)(2,1)S(1)}, u32[]{:S(2)}, u32[]{:S(2)}) collective-permute-start(bf16[256,2048]{1,0:T(8,128)(2,1)S(1)} %collective-permute-done), channel_id=1, source_target_pairs={{0,2},{2,4},{4,6},{6,8},{8,10},{10,12},{12,14},{14,0},{1,3},{3,5},... | collective-permute-start | bytes 3145736 | tf_op jit(solution)/shard_map/ppermute | solution.py:16
  64.6 26.1 %collective-permute-start.2 = (bf16[256,2048]{1,0:T(8,128)(2,1)S(1)}, bf16[256,2048]{1,0:T(8,128)(2,1)S(1)}, u32[]{:S(2)}, u32[]{:S(2)}) collective-permute-start(bf16[256,2048]{1,0:T(8,128)(2,1)S(1)} %collective-permute-done.1), channel_id=1, source_target_pairs={{0,2},{2,4},{4,6},{6,8},{8,10},{10,12},{12,14},{14,0},{1,3},{3,5},... | collective-permute-start | bytes 3145736 | tf_op jit(solution)/shard_map/ppermute | solution.py:16
  90.8 1.0 copy-start.4
  91.7 25.2 %collective-permute-start.3 = (bf16[256,2048]{1,0:T(8,128)(2,1)S(1)}, bf16[256,2048]{1,0:T(8,128)(2,1)S(1)}, u32[]{:S(2)}, u32[]{:S(2)}) collective-permute-start(bf16[256,2048]{1,0:T(8,128)(2,1)S(1)} %collective-permute-done.2), channel_id=1, source_target_pairs={{0,2},{2,4},{4,6},{6,8},{8,10},{10,12},{12,14},{14,0},{1,3},{3,5},... | collective-permute-start | bytes 3145736 | tf_op jit(solution)/shard_map/ppermute | solution.py:16
  116.9 1.0 copy-start.6
  117.9 24.3 %collective-permute-start.4 = (bf16[256,2048]{1,0:T(8,128)(2,1)S(1)}, bf16[256,2048]{1,0:T(8,128)(2,1)S(1)}, u32[]{:S(2)}, u32[]{:S(2)}) collective-permute-start(bf16[256,2048]{1,0:T(8,128)(2,1)S(1)} %collective-permute-done.3), channel_id=1, source_target_pairs={{0,2},{2,4},{4,6},{6,8},{8,10},{10,12},{12,14},{14,0},{1,3},{3,5},... | collective-permute-start | bytes 3145736 | tf_op jit(solution)/shard_map/ppermute | solution.py:16
  142.2 1.0 copy-start.8
  143.1 23.5 %collective-permute-start.5 = (bf16[256,2048]{1,0:T(8,128)(2,1)S(1)}, bf16[256,2048]{1,0:T(8,128)(2,1)}, u32[]{:S(2)}, u32[]{:S(2)}) collective-permute-start(bf16[256,2048]{1,0:T(8,128)(2,1)S(1)} %collective-permute-done.4), channel_id=1, source_target_pairs={{0,2},{2,4},{4,6},{6,8},{8,10},{10,12},{12,14},{14,0},{1,3},{3,5},... | collective-permute-start | bytes 3145736 | tf_op jit(solution)/shard_map/ppermute | solution.py:16
  166.6 22.8 %collective-permute-start.6 = (bf16[256,2048]{1,0:T(8,128)(2,1)}, bf16[256,2048]{1,0:T(8,128)(2,1)}, u32[]{:S(2)}, u32[]{:S(2)}) collective-permute-start(bf16[256,2048]{1,0:T(8,128)(2,1)} %collective-permute-done.5), channel_id=1, source_target_pairs={{0,2},{2,4},{4,6},{6,8},{8,10},{10,12},{12,14},{14,0},{1,3},{3,5},... | collective-permute-start | bytes 3145736 | tf_op jit(solution)/shard_map/ppermute | solution.py:16
  166.6 32.2 %copy-start.5 = (bf16[256,2048]{1,0:T(8,128)(2,1)S(1)}, bf16[256,2048]{1,0:T(8,128)(2,1)}, u32[]{:S(2)}) copy-start(bf16[256,2048]{1,0:T(8,128)(2,1)} %copy-done.4) | copy-start | bytes 3145732
  194.0 13.7 %copy-start.9 = (bf16[256,2048]{1,0:T(8,128)(2,1)S(1)}, bf16[256,2048]{1,0:T(8,128)(2,1)}, u32[]{:S(2)}) copy-start(bf16[256,2048]{1,0:T(8,128)(2,1)} %copy-done.8) | copy-start | bytes 3145732
  196.4 12.4 %copy-start.7 = (bf16[256,2048]{1,0:T(8,128)(2,1)S(1)}, bf16[256,2048]{1,0:T(8,128)(2,1)}, u32[]{:S(2)}) copy-start(bf16[256,2048]{1,0:T(8,128)(2,1)} %copy-done.6) | copy-start | bytes 3145732
  203.0 11.1 %copy-start.15 = (f32[2048]{0:T(1024)S(1)}, f32[2048]{0:T(1024)}, u32[]{:S(2)}) copy-start(f32[2048]{0:T(1024)} %param.9) | copy-start | bytes 24580
  214.0 33.4 %copy-start.11 = (bf16[1,32,16384]{2,1,0:T(8,128)(2,1)S(1)}, bf16[1,32,16384]{2,1,0:T(8,128)(2,1)}, u32[]{:S(2)}) copy-start(bf16[1,32,16384]{2,1,0:T(8,128)(2,1)} %param.13) | copy-start | bytes 3145732
  243.6 25.6 %copy-start.16 = (f32[512]{0:T(512)S(1)}, f32[512]{0:T(512)}, u32[]{:S(2)}) copy-start(f32[512]{0:T(512)} %param.11) | copy-start | bytes 6148
  243.6 23.6 %all-to-all-start = ((bf16[8,32,2048]{2,1,0:T(8,128)(2,1)}), bf16[8,32,2048]{2,1,0:T(8,128)(2,1)S(1)}, u32[]{:S(2)}, u32[]{:S(2)}) async-start(bf16[8,32,2048]{2,1,0:T(8,128)(2,1)} %bitcast.1), calls=%async_computation | async-start | bytes 2097152 | tf_op jit(solution)/shard_map/all_to_all | solution.py:34
  247.7 25.4 %copy-start.12 = (bf16[4,8,128,128]{3,2,1,0:T(8,128)(2,1)}, bf16[4,8,128,128]{3,2,1,0:T(8,128)(2,1)S(1)}, u32[]{:S(2)}) copy-start(bf16[4,8,128,128]{3,2,1,0:T(8,128)(2,1)S(1)} %copy.19) | copy-start | bytes 3145732
  269.1 3.9 copy-start.10
  269.1 3.9 copy-start.14
  276.8 2.0 copy-start.1
  284.9 10.8 %copy-start.13 = (bf16[4,8,128,128]{3,2,1,0:T(8,128)(2,1)S(1)}, bf16[4,8,128,128]{3,2,1,0:T(8,128)(2,1)}, u32[]{:S(2)}) copy-start(bf16[4,8,128,128]{3,2,1,0:T(8,128)(2,1)} %copy-done.12) | copy-start | bytes 3145732
  284.9 30.5 %copy-start.3 = (bf16[1,256,2048]{2,1,0:T(8,128)(2,1)S(1)}, bf16[1,256,2048]{2,1,0:T(8,128)(2,1)}, u32[]{:S(2)}) copy-start(bf16[1,256,2048]{2,1,0:T(8,128)(2,1)} %param.7) | copy-start | bytes 3145732
  288.1 27.2 %all-to-all-start.1 = ((bf16[32,8,2048]{2,0,1:T(8,128)(2,1)}), bf16[32,8,2048]{2,0,1:T(8,128)(2,1)S(1)}, u32[]{:S(2)}, u32[]{:S(2)}) async-start(bf16[32,8,2048]{2,0,1:T(8,128)(2,1)} %copy.14), calls=%async_computation.1 | async-start | bytes 2097152 | tf_op jit(solution)/shard_map/all_to_all | solution.py:65
  291.7 98.0 %all-reduce.3.cloned.1.call-start = ((), (), s32[]{:S(2)}) async-start(), calls=%async_computation.5 | async-start | bytes 524288 | tf_op jit(solution)/shard_map/psum | solution.py:56
  299.8 243.4 %reduce-scatter.2.cloned.1.call-start = ((), (), s32[]{:S(2)}) async-start(), calls=%async_computation.4 | async-start | bytes 9437184 | tf_op jit(solution)/shard_map/reduce_scatter | solution.py:75
Sparse Core Ops, SparseCore 0:
  9.6 97.7 all-gather.1
  299.9 89.6 all-reduce.2
  393.3 149.8 reduce-scatter.1
